TPU v7x, 256 devices: a whole 4x4x8 slice. The times are simulated.
256 devices in a mesh: row: 8 (over z), col: 32 (over y, x, core).
Axes of the slice: x: 4, y: 4, z: 8, core: 2. Of those that a mesh axis runs over, the one named last changes fastest.
Arguments:
- amps: bfloat16 [384, 131072], P('row', 'col'), may hold values from -6 to 6
- integrals: bfloat16 [131072, 8192], P('col', 'row'), may hold values from -0.046875 to 0.046875
- cd_first: int32 [131072], P('col'), may hold values from 0 to 2399
- cd_second: int32 [131072], P('col'), may hold values from 0 to 2399
- ab_first: int32 [8192], P('row'), may hold values from 0 to 2399
- ab_second: int32 [8192], P('row'), may hold values from 0 to 2399
- occ_first: int32 [384], P('col'), may hold values from 0 to 199
- occ_second: int32 [384], P('col'), may hold values from 0 to 199
- virt_irrep: int32 [2400], replicated, may hold values from 0 to 7
- occ_energy: float32 [200], replicated, may hold values from -2 to -0.5
- virt_energy: float32 [2400], replicated, may hold values from 0.2 to 3
Outputs:
- update: float32 [384, 8192], P('col', 'row')
All inputs are finite; a program needn't handle non-finite values.
Results may differ from a plain program's by a relative error of at most 0.0003.
Values may be sent and summed in bfloat16 or wider, within the bound.
No kernel may reach another device: no remote copies, remote signals or barrier semaphores. Data moves between devices by JAX's collectives and lax.ppermute only.
A program may use at most 64 MiB of HBM per device.

v0:
```python
import jax
import jax.numpy as jnp
from jax import lax
from jax.sharding import PartitionSpec as P


def table_lookup(values_table, positions):
    row_width = 64
    row_count = -(-values_table.shape[0] // row_width)
    padded_table = jnp.pad(
        values_table, (0, row_count * row_width - values_table.shape[0])
    ).reshape(row_count, row_width)
    high_hot = (
        (positions // row_width)[:, None] == jnp.arange(row_count, dtype=jnp.int32)[None, :]
    ).astype(jnp.float32)
    low_hot = (
        (positions % row_width)[:, None] == jnp.arange(row_width, dtype=jnp.int32)[None, :]
    ).astype(jnp.float32)
    picked = jnp.dot(
        high_hot, padded_table, precision=lax.Precision.HIGHEST, preferred_element_type=jnp.float32
    )
    return jnp.sum(picked * low_hot, axis=1)


def irrep_of(labels_float, first_orb, second_orb):
    first_label = table_lookup(labels_float, first_orb).astype(jnp.int32)
    second_label = table_lookup(labels_float, second_orb).astype(jnp.int32)
    return jnp.bitwise_xor(first_label, second_label)


def on_device(
    amps,
    integrals,
    cd_first,
    cd_second,
    ab_first,
    ab_second,
    occ_first,
    occ_second,
    virt_irrep,
    occ_energy,
    virt_energy,
):
    labels_float = virt_irrep.astype(jnp.float32)
    irrep_cd = irrep_of(labels_float, cd_first, cd_second)
    irrep_ab = irrep_of(labels_float, ab_first, ab_second)
    masked = jnp.where(irrep_cd[:, None] == irrep_ab[None, :], integrals, jnp.zeros_like(integrals))
    partial_sums = jnp.dot(
        lax.all_gather(amps, "row", axis=0, tiled=True), masked, preferred_element_type=jnp.float32
    )
    own_rows = occ_first.shape[0]
    summed = lax.psum(partial_sums, "col")
    ladder = lax.dynamic_slice_in_dim(summed, lax.axis_index("col") * own_rows, own_rows, 0)
    virt_part = table_lookup(virt_energy, ab_first) + table_lookup(virt_energy, ab_second)
    occ_part = table_lookup(occ_energy, occ_first) + table_lookup(occ_energy, occ_second)
    denom = virt_part[None, :] - occ_part[:, None]
    return ladder / denom


def solution(mesh):
    in_specs = (
        P("row", "col"),
        P("col", "row"),
        P("col"),
        P("col"),
        P("row"),
        P("row"),
        P("col"),
        P("col"),
        P(),
        P(),
        P(),
    )
    out_specs = P("col", "row")
    return jax.shard_map(
        on_device, mesh=mesh, in_specs=in_specs, out_specs=out_specs, check_vma=False
    )
```

profile of v0, /device:TPU:6, one launch (start us, length us, event | category | flops | bytes accessed | tf_op | source)
XLA Modules:
  0.0 190.4 jit_solution(7204045527473177920)
XLA Ops:
  6.5 0.0 all-gather.2.cloned.1.call-start
  6.5 0.7 all-gather.2.cloned.1.call-update
  7.3 0.0 all-reduce.5.cloned.1.call-start
  7.3 0.7 convert_element_type.57
  8.0 0.1 reshape.50
  8.1 0.7 add_select_fusion.5
  8.8 0.6 fusion.8
  9.4 0.7 add_select_fusion.7
  10.1 0.6 fusion.7
  10.7 0.7 add_select_fusion.2
  11.4 0.7 fusion.5
  12.1 0.7 add_select_fusion
  12.8 0.7 fusion.6
  13.5 0.0 copy-start.2
  13.6 0.0 copy-start.1
  13.6 0.0 copy-start
  13.6 0.0 copy-start.3
  13.6 43.5 %all-gather.2.cloned.1.call-done = bf16[384,4096]{1,0:T(8,128)(2,1)} async-done(((bf16[48,4096]{1,0:T(8,128)(2,1)}), bf16[384,4096]{1,0:T(8,128)(2,1)}) %all-gather.2.cloned.1.call-update) | async-done | bytes 3145744 | tf_op jit(solution)/shard_map/all_gather | solution.py:49
  57.1 9.0 %fusion.4 = f32[384,1024]{1,0:T(8,128)} fusion(bf16[384,4096]{1,0:T(8,128)(2,1)} %all-gather.2.cloned.1.call-done, bf16[4096,1024]{1,0:T(8,128)(2,1)} %param.12, s32[1024]{0:T(1024)S(1)} %convert_xor_fusion.1, s32[4096]{0:T(1024)S(1)} %convert_xor_fusion), kind=kOutput, calls=%fused_computation.7 | convolution fusion | flops 3229614080 | bytes 13127680 | tf_op jit(solution)/shard_map/dot_general | solution.py:48
  66.1 0.0 all-reduce.5.cloned.1.call-update
  66.1 0.0 copy-done.2
  66.1 0.0 copy-done.1
  66.2 0.1 reshape.52
  66.2 0.0 copy-done
  66.2 0.1 reshape.51
  66.3 0.3 fusion.11
  66.6 0.0 copy-done.3
  66.6 0.3 fusion.12
  67.0 0.6 fusion.10
  67.5 0.6 fusion.9
  68.1 113.8 %all-reduce.5.cloned.1.call-done = f32[384,1024]{1,0:T(8,128)} async-done(((f32[384,1024]{1,0:T(8,128)}), f32[384,1024]{1,0:T(8,128)}) %all-reduce.5.cloned.1.call-update) | async-done | bytes 1572880 | tf_op jit(solution)/shard_map/psum | solution.py:52
  181.9 1.6 subtract_divide_fusion
  (9 shorter events, 0.1 us)
Async XLA Ops:
  6.5 50.5 %all-gather.2.cloned.1.call-start = ((), (), s32[]{:S(2)}) async-start(), calls=%async_computation | async-start | bytes 3538944 | tf_op jit(solution)/shard_map/all_gather | solution.py:49
  7.3 174.7 %all-reduce.5.cloned.1.call-start = ((), (), s32[]{:S(2)}) async-start(), calls=%async_computation.1 | async-start | bytes 3145728 | tf_op jit(solution)/shard_map/psum | solution.py:52
  13.5 52.5 %copy-start.2 = (s32[12]{0:T(128)S(1)}, s32[12]{0:T(128)}, u32[]{:S(2)}) copy-start(s32[12]{0:T(128)} %param.17) | copy-start | bytes 148
  13.6 52.6 %copy-start.1 = (f32[200]{0:T(256)S(1)}, f32[200]{0:T(256)}, u32[]{:S(2)}) copy-start(f32[200]{0:T(256)} %param.20) | copy-start | bytes 2404
  13.6 52.7 %copy-start = (f32[2400]{0:T(1024)S(1)}, f32[2400]{0:T(1024)}, u32[]{:S(2)}) copy-start(f32[2400]{0:T(1024)} %param.21) | copy-start | bytes 28804
  13.6 53.0 %copy-start.3 = (s32[12]{0:T(128)S(1)}, s32[12]{0:T(128)}, u32[]{:S(2)}) copy-start(s32[12]{0:T(128)} %param.18) | copy-start | bytes 148
Sparse Core Ops, SparseCore 0:
  9.1 47.8 all-gather.1
  66.2 115.6 all-reduce.4
where the time goes:
time: 191 us; the launch traced here: 190 us
  waiting for transfers between devices  158 us (83%)
  between operations  13.5 us (7%)
  matrix products  13.3 us (7%)
  other arithmetic  5.24 us (3%)
    psum x1, waiting for transfers between devices, on_device(): summed = lax.psum(partial_sums, 'col')  114 us
    all_gather x1, waiting for transfers between devices, on_device(): lax.all_gather(amps, 'row', axis=0, tiled=True)  43.5 us
    dot_general x1, matrix products, on_device(): jnp.dot(lax.all_gather(amps, 'row', axis=0, tiled=True), masked, preferre...  9 us
    dot_general x8, matrix products, table_lookup(): jnp.dot(high_hot, padded_table, precision=lax.Precision.HIGHEST, preferre...  4.28 us
  transfers between devices with their start and end apart: 2, of which 2 were waited for; matrix products, arithmetic and copies ran while one was open for 4% of the time, Pallas kernels for 0%

commit v1 on v0

--- a/solution.py
+++ b/solution.py
@@ -2,6 +2,27 @@
 import jax.numpy as jnp
 from jax import lax
 from jax.sharding import PartitionSpec as P
+
+
+def ring_gather(x, axis, dim):
+    devices, here, rows = (lax.axis_size(axis), lax.axis_index(axis), x.shape[dim])
+    right = [(i, (i + 1) % devices) for i in range(devices)]
+    downward = [(i, (i - 1) % devices) for i in range(devices)]
+    filled = jnp.zeros((*x.shape[:dim], devices * rows, *x.shape[dim + 1 :]), x.dtype)
+    filled = lax.dynamic_update_slice_in_dim(filled, x, here * rows, axis=dim)
+    from_left = from_right = x
+    halfway = devices // 2
+    for step in range(1, halfway + 1):
+        from_left = lax.ppermute(from_left, axis, right)
+        filled = lax.dynamic_update_slice_in_dim(
+            filled, from_left, (here - step) % devices * rows, axis=dim
+        )
+        if step < devices - halfway:
+            from_right = lax.ppermute(from_right, axis, downward)
+            filled = lax.dynamic_update_slice_in_dim(
+                filled, from_right, (here + step) % devices * rows, axis=dim
+            )
+    return filled
 
 
 def table_lookup(values_table, positions):
@@ -45,9 +66,7 @@
     irrep_cd = irrep_of(labels_float, cd_first, cd_second)
     irrep_ab = irrep_of(labels_float, ab_first, ab_second)
     masked = jnp.where(irrep_cd[:, None] == irrep_ab[None, :], integrals, jnp.zeros_like(integrals))
-    partial_sums = jnp.dot(
-        lax.all_gather(amps, "row", axis=0, tiled=True), masked, preferred_element_type=jnp.float32
-    )
+    partial_sums = jnp.dot(ring_gather(amps, "row", 0), masked, preferred_element_type=jnp.float32)
     own_rows = occ_first.shape[0]
     summed = lax.psum(partial_sums, "col")
     ladder = lax.dynamic_slice_in_dim(summed, lax.axis_index("col") * own_rows, own_rows, 0)

time: 191 us -> 183 us (0.958)
  waiting for transfers between devices: 158 us -> 143 us
  starting transfers between devices: 0.04 us -> 12.3 us
  matrix products: 13.3 us -> 9.04 us
    all_gather x1 -> x0, waiting for transfers between devices: 43.5 us -> none  [on_device(): lax.all_gather(amps, 'row', axis=0, tiled=True)]
    ppermute x0 -> x7, waiting for transfers between devices: none -> 28.3 us  [the longest x4 28.3 us: ring_gather(): from_left = lax.ppermute(from_left, axis, right)]
    ppermute x0 -> x7, starting transfers between devices: none -> 12.3 us  [the longest x3 10.4 us: ring_gather(): from_right = lax.ppermute(from_right, axis, downward)]
    dot_general x1, matrix products: 9 us -> 4.75 us  [on_device(): jnp.dot(ring_gather(amps, 'row', 0), masked, preferred_element_type=jnp.f...]
  transfers between devices with their start and end apart: 2 -> 8, of which waited for: 2 -> 5; matrix products, arithmetic and copies ran while one was open for 4% -> 4% of each run, Pallas kernels for 0% -> 0%
where the time goes in v1:
time: 183 us
  waiting for transfers between devices  143 us (78%)
  between operations  13.7 us (7%)
  starting transfers between devices  12.3 us (7%)
  matrix products  9.04 us (5%)
  other arithmetic  4.55 us (2%)
    psum x1, waiting for transfers between devices, on_device(): summed = lax.psum(partial_sums, 'col')  114 us
    ppermute x4, waiting for transfers between devices, ring_gather(): from_left = lax.ppermute(from_left, axis, right)  28.3 us
    ppermute x3, starting transfers between devices, ring_gather(): from_right = lax.ppermute(from_right, axis, downward)  10.4 us
    dot_general x1, matrix products, on_device(): jnp.dot(ring_gather(amps, 'row', 0), masked, preferred_element_type=jnp.f...  4.75 us
    dot_general x8, matrix products, table_lookup(): jnp.dot(high_hot, padded_table, precision=lax.Precision.HIGHEST, preferre...  4.29 us
  transfers between devices with their start and end apart: 8, of which 5 were waited for; matrix products, arithmetic and copies ran while one was open for 4% of the time, Pallas kernels for 0%

profile of v1, /device:TPU:6, one launch (start us, length us, event | category | flops | bytes accessed | tf_op | source)
XLA Modules:
  0.0 183.1 jit_solution(5939161619436612491)
XLA Ops:
  6.5 1.9 %collective-permute-start = (bf16[48,4096]{1,0:T(8,128)(2,1)}, bf16[48,4096]{1,0:T(8,128)(2,1)S(1)}, u32[]{:S(2)}, u32[]{:S(2)}) collective-permute-start(bf16[48,4096]{1,0:T(8,128)(2,1)} %param.11), channel_id=1, source_target_pairs={{0,32},{32,64},{64,96},{96,128},{128,160},{160,192},{192,224},{224... | collective-permute-start | bytes 1179656 | tf_op jit(solution)/shard_map/ppermute | solution.py:16
  8.5 3.9 %collective-permute-start.1 = (bf16[48,4096]{1,0:T(8,128)(2,1)}, bf16[48,4096]{1,0:T(8,128)(2,1)S(1)}, u32[]{:S(2)}, u32[]{:S(2)}) collective-permute-start(bf16[48,4096]{1,0:T(8,128)(2,1)} %param.11), channel_id=1, source_target_pairs={{0,224},{32,0},{64,32},{96,64},{128,96},{160,128},{192,160},{224,1... | collective-permute-start | bytes 1179656 | tf_op jit(solution)/shard_map/ppermute | solution.py:21
  12.4 0.7 convert_element_type.57
  13.1 0.1 reshape.50
  13.2 0.7 add_select_fusion.2
  13.9 0.7 add_select_fusion
  14.7 0.7 add_select_fusion.5
  15.4 0.0 copy-start
  15.4 0.6 fusion.6
  16.0 0.6 fusion.7
  16.6 0.7 fusion.4
  17.3 0.7 fusion.5
  18.0 0.0 copy-start.5
  18.0 0.4 broadcast_in_dim.4
  18.4 3.3 %collective-permute-done = bf16[48,4096]{1,0:T(8,128)(2,1)S(1)} collective-permute-done((bf16[48,4096]{1,0:T(8,128)(2,1)}, bf16[48,4096]{1,0:T(8,128)(2,1)S(1)}, u32[]{:S(2)}, u32[]{:S(2)}) %collective-permute-start) | collective-permute-done | bytes 393248 | tf_op jit(solution)/shard_map/ppermute | solution.py:16
  21.7 3.2 %collective-permute-start.3 = (bf16[48,4096]{1,0:T(8,128)(2,1)S(1)}, bf16[48,4096]{1,0:T(8,128)(2,1)S(1)}, u32[]{:S(2)}, u32[]{:S(2)}) collective-permute-start(bf16[48,4096]{1,0:T(8,128)(2,1)S(1)} %collective-permute-done.1), channel_id=1, source_target_pairs={{0,224},{32,0},{64,32},{96,64},{128,96},{160,128},{192,160},{224,1... | collective-permute-start | bytes 1179656 | tf_op jit(solution)/shard_map/ppermute | solution.py:21
  25.0 8.2 %collective-permute-done.2 = bf16[48,4096]{1,0:T(8,128)(2,1)S(1)} collective-permute-done((bf16[48,4096]{1,0:T(8,128)(2,1)S(1)}, bf16[48,4096]{1,0:T(8,128)(2,1)S(1)}, u32[]{:S(2)}, u32[]{:S(2)}) %collective-permute-start.2) | collective-permute-done | bytes 393248 | tf_op jit(solution)/shard_map/ppermute | solution.py:16
  33.2 3.2 %collective-permute-start.5 = (bf16[48,4096]{1,0:T(8,128)(2,1)S(1)}, bf16[48,4096]{1,0:T(8,128)(2,1)S(1)}, u32[]{:S(2)}, u32[]{:S(2)}) collective-permute-start(bf16[48,4096]{1,0:T(8,128)(2,1)S(1)} %collective-permute-done.3), channel_id=1, source_target_pairs={{0,224},{32,0},{64,32},{96,64},{128,96},{160,128},{192,160},{224,1... | collective-permute-start | bytes 1179656 | tf_op jit(solution)/shard_map/ppermute | solution.py:21
  36.5 7.3 %collective-permute-done.4 = bf16[48,4096]{1,0:T(8,128)(2,1)S(1)} collective-permute-done((bf16[48,4096]{1,0:T(8,128)(2,1)S(1)}, bf16[48,4096]{1,0:T(8,128)(2,1)S(1)}, u32[]{:S(2)}, u32[]{:S(2)}) %collective-permute-start.4) | collective-permute-done | bytes 393248 | tf_op jit(solution)/shard_map/ppermute | solution.py:16
  43.9 9.6 %collective-permute-done.6 = bf16[48,4096]{1,0:T(8,128)(2,1)S(1)} collective-permute-done((bf16[48,4096]{1,0:T(8,128)(2,1)S(1)}, bf16[48,4096]{1,0:T(8,128)(2,1)S(1)}, u32[]{:S(2)}, u32[]{:S(2)}) %collective-permute-start.6) | collective-permute-done | bytes 393248 | tf_op jit(solution)/shard_map/ppermute | solution.py:16
  53.5 0.0 copy-start.2
  53.6 0.0 copy-start.3
  53.6 4.8 %fusion = f32[384,1024]{1,0:T(8,128)} fusion(bf16[384,4096]{1,0:T(8,128)(2,1)S(1)} %constant_dynamic-update-slice_fusion, bf16[4096,1024]{1,0:T(8,128)(2,1)S(1)} %copy-done.5, s32[1024]{0:T(1024)S(1)} %convert_xor_fusion.1, s32[4096]{0:T(1024)S(1)} %convert_xor_fusion), kind=kOutput, calls=%fused_computation.1 | convolution fusion | flops 3229614080 | bytes 13127680 | tf_op jit(solution)/shard_map/dot_general | solution.py:69
  58.3 0.0 all-reduce.5.cloned.1.call-update
  58.4 0.1 reshape.51
  58.5 0.1 reshape.52
  58.5 0.6 fusion.8
  59.1 0.6 fusion.9
  59.8 0.3 fusion.10
  60.1 0.3 fusion.11
  60.4 114.2 %all-reduce.5.cloned.1.call-done = f32[384,1024]{1,0:T(8,128)} async-done(((f32[384,1024]{1,0:T(8,128)}), f32[384,1024]{1,0:T(8,128)}) %all-reduce.5.cloned.1.call-update) | async-done | bytes 1572880 | tf_op jit(solution)/shard_map/psum | solution.py:71
  174.6 1.6 subtract_divide_fusion
  (31 shorter events, 0.3 us)
Async XLA Ops:
  6.5 168.1 %all-reduce.5.cloned.1.call-start = ((), (), s32[]{:S(2)}) async-start(), calls=%async_computation | async-start | bytes 3145728 | tf_op jit(solution)/shard_map/psum | solution.py:71
  6.5 15.2 %collective-permute-start = (bf16[48,4096]{1,0:T(8,128)(2,1)}, bf16[48,4096]{1,0:T(8,128)(2,1)S(1)}, u32[]{:S(2)}, u32[]{:S(2)}) collective-permute-start(bf16[48,4096]{1,0:T(8,128)(2,1)} %param.11), channel_id=1, source_target_pairs={{0,32},{32,64},{64,96},{96,128},{128,160},{160,192},{192,224},{224... | collective-permute-start | bytes 1179656 | tf_op jit(solution)/shard_map/ppermute | solution.py:16
  8.5 13.3 %collective-permute-start.1 = (bf16[48,4096]{1,0:T(8,128)(2,1)}, bf16[48,4096]{1,0:T(8,128)(2,1)S(1)}, u32[]{:S(2)}, u32[]{:S(2)}) collective-permute-start(bf16[48,4096]{1,0:T(8,128)(2,1)} %param.11), channel_id=1, source_target_pairs={{0,224},{32,0},{64,32},{96,64},{128,96},{160,128},{192,160},{224,1... | collective-permute-start | bytes 1179656 | tf_op jit(solution)/shard_map/ppermute | solution.py:21
  15.4 3.0 %copy-start = (bf16[48,4096]{1,0:T(8,128)(2,1)S(1)}, bf16[48,4096]{1,0:T(8,128)(2,1)}, u32[]{:S(2)}) copy-start(bf16[48,4096]{1,0:T(8,128)(2,1)} %param.11) | copy-start | bytes 1179652
  18.0 35.5 %copy-start.5 = (bf16[4096,1024]{1,0:T(8,128)(2,1)S(1)}, bf16[4096,1024]{1,0:T(8,128)(2,1)}, u32[]{:S(2)}) copy-start(bf16[4096,1024]{1,0:T(8,128)(2,1)} %param.12) | copy-start | bytes 25165828
  21.7 11.5 %collective-permute-start.2 = (bf16[48,4096]{1,0:T(8,128)(2,1)S(1)}, bf16[48,4096]{1,0:T(8,128)(2,1)S(1)}, u32[]{:S(2)}, u32[]{:S(2)}) collective-permute-start(bf16[48,4096]{1,0:T(8,128)(2,1)S(1)} %collective-permute-done), channel_id=1, source_target_pairs={{0,32},{32,64},{64,96},{96,128},{128,160},{160,192},{192,224},{224... | collective-permute-start | bytes 1179656 | tf_op jit(solution)/shard_map/ppermute | solution.py:16
  21.7 11.5 %collective-permute-start.3 = (bf16[48,4096]{1,0:T(8,128)(2,1)S(1)}, bf16[48,4096]{1,0:T(8,128)(2,1)S(1)}, u32[]{:S(2)}, u32[]{:S(2)}) collective-permute-start(bf16[48,4096]{1,0:T(8,128)(2,1)S(1)} %collective-permute-done.1), channel_id=1, source_target_pairs={{0,224},{32,0},{64,32},{96,64},{128,96},{160,128},{192,160},{224,1... | collective-permute-start | bytes 1179656 | tf_op jit(solution)/shard_map/ppermute | solution.py:21
  33.2 10.6 %collective-permute-start.4 = (bf16[48,4096]{1,0:T(8,128)(2,1)S(1)}, bf16[48,4096]{1,0:T(8,128)(2,1)S(1)}, u32[]{:S(2)}, u32[]{:S(2)}) collective-permute-start(bf16[48,4096]{1,0:T(8,128)(2,1)S(1)} %collective-permute-done.2), channel_id=1, source_target_pairs={{0,32},{32,64},{64,96},{96,128},{128,160},{160,192},{192,224},{224... | collective-permute-start | bytes 1179656 | tf_op jit(solution)/shard_map/ppermute | solution.py:16
  33.2 10.6 %collective-permute-start.5 = (bf16[48,4096]{1,0:T(8,128)(2,1)S(1)}, bf16[48,4096]{1,0:T(8,128)(2,1)S(1)}, u32[]{:S(2)}, u32[]{:S(2)}) collective-permute-start(bf16[48,4096]{1,0:T(8,128)(2,1)S(1)} %collective-permute-done.3), channel_id=1, source_target_pairs={{0,224},{32,0},{64,32},{96,64},{128,96},{160,128},{192,160},{224,1... | collective-permute-start | bytes 1179656 | tf_op jit(solution)/shard_map/ppermute | solution.py:21
  43.8 9.7 %collective-permute-start.6 = (bf16[48,4096]{1,0:T(8,128)(2,1)S(1)}, bf16[48,4096]{1,0:T(8,128)(2,1)S(1)}, u32[]{:S(2)}, u32[]{:S(2)}) collective-permute-start(bf16[48,4096]{1,0:T(8,128)(2,1)S(1)} %collective-permute-done.4), channel_id=1, source_target_pairs={{0,32},{32,64},{64,96},{96,128},{128,160},{160,192},{192,224},{224... | collective-permute-start | bytes 1179656 | tf_op jit(solution)/shard_map/ppermute | solution.py:16
  53.5 4.8 %copy-start.1 = (f32[2400]{0:T(1024)S(1)}, f32[2400]{0:T(1024)}, u32[]{:S(2)}) copy-start(f32[2400]{0:T(1024)} %param.21) | copy-start | bytes 28804
  53.5 4.9 %copy-start.2 = (f32[200]{0:T(256)S(1)}, f32[200]{0:T(256)}, u32[]{:S(2)}) copy-start(f32[200]{0:T(256)} %param.20) | copy-start | bytes 2404
  53.6 6.2 %copy-start.3 = (s32[12]{0:T(128)S(1)}, s32[12]{0:T(128)}, u32[]{:S(2)}) copy-start(s32[12]{0:T(128)} %param.18) | copy-start | bytes 148
  53.6 6.2 %copy-start.4 = (s32[12]{0:T(128)S(1)}, s32[12]{0:T(128)}, u32[]{:S(2)}) copy-start(s32[12]{0:T(128)} %param.17) | copy-start | bytes 148
Sparse Core Ops, SparseCore 0:
  58.5 116.0 all-reduce.4
